TPU v7x, 32 devices: a whole 2x2x4 slice. The times are simulated.
32 devices in a mesh: seq: 1, ctx: 8 (over y, x, core), head: 4 (over z).
Axes of the slice: x: 2, y: 2, z: 4, core: 2. Of those that a mesh axis runs over, the one named last changes fastest.
Arguments:
- queries: bfloat16 [3072, 4096], P(('seq', 'ctx'), 'head'), may hold values from -6 to 6
- keys: bfloat16 [3072, 4096], P(('seq', 'ctx'), 'head'), may hold values from -6 to 6
- values: bfloat16 [3072, 4096], P(('seq', 'ctx'), 'head'), may hold values from -6 to 6
- grad_out: bfloat16 [3072, 4096], P(('seq', 'ctx'), 'head'), may hold values from -6 to 6
Outputs:
- attn_out: bfloat16 [3072, 4096], P(('seq', 'ctx'), 'head')
- grad_queries: bfloat16 [3072, 4096], P(('seq', 'ctx'), 'head')
- grad_keys: bfloat16 [3072, 4096], P(('seq', 'ctx'), 'head')
- grad_values: bfloat16 [3072, 4096], P(('seq', 'ctx'), 'head')
All inputs are finite; a program needn't handle non-finite values.
Results may differ from a plain program's by a relative error of at most 0.0051.
Values sent between devices are 32-bit elements; how exact they have to be, the bound alone decides.
A program may use at most 64 MiB of HBM per device.

v0:
```python
import functools
import math

import jax
import jax.numpy as jnp
from jax import lax
from jax.experimental import pallas as pl
from jax.experimental.pallas import tpu as pltpu
from jax.sharding import PartitionSpec as P

DH = 128
F32 = jnp.float32
BF16 = jnp.bfloat16
PUT_PIECES = 3


def dot_nn(a, b):
    return lax.dot_general(a, b, (((1,), (0,)), ((), ())), preferred_element_type=F32)


def dot_nt(a, b):
    return lax.dot_general(a, b, (((1,), (1,)), ((), ())), preferred_element_type=F32)


def dot_tn(a, b):
    return lax.dot_general(a, b, (((0,), (0,)), ((), ())), preferred_element_type=F32)


def kernel(factor, q_hbm, k_hbm, v_hbm, g_hbm, attn_ref, gq_ref, gk_ref, gv_ref,
           ops, acc, give, mine, pre, chip, xin, ysum, yin, fin, fin_in, states,
           in_sem, pre_s, pre_r, x_s, x_r, y_s, y_r, f_s, f_r):
    me = lax.axis_index("ctx")
    core = me % 2
    xb = (me // 2) % 2
    yb = me // 4
    end = xb == yb
    mid = xb != yb
    partner = me + 1 - 2 * core
    x_dev = me + 2 - 4 * xb
    y_dev = me + 4 - 8 * yb
    tok, feat = q_hbm.shape
    half = feat // 2
    hh = half // DH

    barrier = pltpu.get_barrier_semaphore()
    for dev in (partner, x_dev, y_dev):
        pl.semaphore_signal(barrier, inc=1, device_id={"ctx": dev}, device_id_type=pl.DeviceIdType.MESH)

    cols_of = (pl.multiple_of((1 - core) * half, half), pl.multiple_of(core * half, half))
    i_k, i_v, i_q, i_g = 2 * yb, 2 * yb + 1, 2 - 2 * yb, 3 - 2 * yb

    def fetch(op, slot, ref):
        return pltpu.make_async_copy(ref.at[:, pl.ds(cols_of[slot], half)], ops.at[op, slot], in_sem.at[op, slot])

    for role in (0, 1):
        @pl.when(yb == role)
        def _():
            refs = (k_hbm, v_hbm, q_hbm, g_hbm) if role == 0 else (q_hbm, g_hbm, k_hbm, v_hbm)
            for r in (0, 1):
                for slot in (0, 1):
                    for op in (2 * r, 2 * r + 1):
                        fetch(op, slot, refs[op]).start()

    def remote(src, dst, ss, rs, dev):
        return pltpu.make_async_remote_copy(
            src_ref=src, dst_ref=dst, send_sem=ss, recv_sem=rs,
            device_id={"ctx": dev}, device_id_type=pl.DeviceIdType.MESH)

    def pre_copy(r, h):
        return remote(give.at[r, h], pre.at[r, h], pre_s.at[r, h], pre_r.at[r, h], partner)

    def x_copy(src, i):
        return remote(src, xin.at[i], x_s.at[i], x_r.at[i], x_dev)

    def y_copy(h, src=None):
        return remote(ysum.at[h] if src is None else src, yin.at[h], y_s.at[h], y_r.at[h], y_dev)

    def fin_copy(r, h):
        return remote(fin.at[r, h], fin_in.at[r, h], f_s.at[r, h], f_r.at[r, h], partner)

    def wait_ops(r, slot):
        fetch(2 * r, slot, q_hbm).wait()
        fetch(2 * r + 1, slot, q_hbm).wait()

    def head(op, slot, h):
        return ops[op, slot, :, h * DH:(h + 1) * DH]

    def local_state(r, slot, h):
        return dot_tn(head(2 * r, slot, h), head(2 * r + 1, slot, h))

    order = (2, 3, 0, 1)

    def states_of(r, first, send):
        wait_ops(r, 0)
        for h in order:
            give[r, h] = local_state(r, 0, h)
            if first and h == order[0]:
                pl.semaphore_wait(barrier, 3)
            pre_copy(r, h).start()
        wait_ops(r, 1)
        for h in order:
            mine[r, h] = local_state(r, 1, h)
        for h in order:
            pre_copy(r, h).wait_recv()
            chip[r, h] = mine[r, h] + pre[r, h]
            send(h)

    def send_p(h):
        @pl.when(end)
        def _():
            x_copy(chip.at[0, h], h).start()

        if h >= 2:
            @pl.when(mid)
            def _():
                x_copy(chip.at[0, h], hh + h - 2).start()
        else:
            y_copy(h, chip.at[0, h]).start()

    def send_r(h):
        if h >= 2:
            @pl.when(mid)
            def _():
                x_copy(chip.at[1, h], h).start()

    states_of(0, True, send_p)
    states_of(1, False, send_r)

    def adds_pre(r):
        return (core + yb + r) % 2 == 1

    def finish_state(r, h, base):
        follows = adds_pre(r)
        zero = jnp.zeros((DH, DH), F32)
        own = jnp.where(follows, pre[r, h], zero)
        other = jnp.where(follows, zero, mine[r, h])
        if base is not None:
            own, other = own + base, other + base
        states[r, 1, h] = own.astype(BF16)
        fin[r, h] = other
        fin_copy(r, h).start()

    @pl.when(end)
    def _():
        for h in range(hh):
            finish_state(0, h, None)

    rows = lax.broadcasted_iota(jnp.int32, (tok, tok), 0)
    columns = lax.broadcasted_iota(jnp.int32, (tok, tok), 1)

    def intra(slot, h):
        q, k, v, g = head(i_q, slot, h), head(i_k, slot, h), head(i_v, slot, h), head(i_g, slot, h)
        causal = columns <= rows
        sc = jnp.where(causal, dot_nt(q, k), 0.0).astype(BF16)
        ds = jnp.where(causal, dot_nt(g, v), 0.0).astype(BF16)
        acc[0, 0, slot, h] = dot_nn(sc, v)
        acc[0, 1, slot, h] = dot_nn(ds, k)
        acc[1, 0, slot, h] = dot_tn(sc, g)
        acc[1, 1, slot, h] = dot_tn(ds, q)

    def apply(r, slot, h):
        state = states[r, slot, h]
        kind = (yb + r) % 2
        left = ops[2 - 2 * r, slot, :, pl.ds(pl.multiple_of(h * DH, DH), DH)]
        right = ops[3 - 2 * r, slot, :, pl.ds(pl.multiple_of(h * DH, DH), DH)]
        one = ((acc[kind, 0, slot, h] + dot_nn(left, state)) * factor).astype(BF16)
        two = ((acc[kind, 1, slot, h] + dot_nt(right, state)) * factor).astype(BF16)
        at = pl.ds(pl.multiple_of(cols_of[slot] + h * DH, DH), DH)

        @pl.when(kind == 0)
        def _():
            attn_ref[:, at] = one
            gq_ref[:, at] = two

        @pl.when(kind == 1)
        def _():
            gv_ref[:, at] = one
            gk_ref[:, at] = two

    def take_final(r, h):
        fin_copy(r, h).wait_recv()
        states[r, 0, h] = fin_in[r, h].astype(BF16)
        apply(r, 0, h)

    def middle_p(h):
        x_copy(chip.at[0, h], h).wait_recv()
        came = xin[h]
        if h >= 2:
            ysum[h] = chip[0, h] + came
            y_copy(h).start()
        finish_state(0, h, came)

    def end_p(i):
        x_copy(chip.at[0, i], hh + i).wait_recv()
        ysum[2 + i] = chip[0, 2 + i] + xin[hh + i]
        y_copy(2 + i).start()

    def end_pass(i):
        y_copy(i).wait_recv()
        x_copy(yin.at[i], hh + i).start()

    def middle_pass(i):
        y_copy(i).wait_recv()
        ysum[i] = chip[1, i] + yin[i]
        x_copy(ysum.at[i], i).start()

    def end_r(h):
        if h >= 2:
            y_copy(h).wait_recv()
        x_copy(chip.at[0, h], h).wait_recv()
        finish_state(1, h, xin[h] + yin[h])

    def middle_r(h):
        if h >= 2:
            y_copy(h).wait_recv()
            finish_state(1, h, yin[h])
        else:
            x_copy(chip.at[0, h], hh + h).wait_recv()
            finish_state(1, h, yin[h] + xin[hh + h])

    def by_place(at_end, at_mid):
        pl.when(end)(at_end)
        pl.when(mid)(at_mid)

    intra(0, 0)
    intra(0, 1)
    by_place(lambda: end_p(0), lambda: middle_p(2))
    by_place(lambda: end_pass(0), lambda: middle_pass(0))
    intra(0, 2)
    by_place(lambda: end_p(1), lambda: middle_p(3))
    by_place(lambda: end_pass(1), lambda: middle_pass(1))
    for h in (3,):
        intra(0, h)
    for h in range(hh):
        intra(1, h)
    pl.when(mid)(lambda: middle_p(0))
    pl.when(mid)(lambda: middle_p(1))
    for h in (2, 3, 0, 1):
        apply(0, 1, h)
    for h in (2, 3):
        by_place(lambda: end_r(h), lambda: middle_r(h))
    for h in (2, 3, 0, 1):
        take_final(0, h)
    apply(1, 1, 2)
    apply(1, 1, 3)
    by_place(lambda: end_r(0), lambda: middle_r(0))
    take_final(1, 2)
    take_final(1, 3)
    apply(1, 1, 0)
    by_place(lambda: end_r(1), lambda: middle_r(1))
    take_final(1, 0)
    apply(1, 1, 1)
    take_final(1, 1)

    for r in (0, 1):
        for h in range(hh):
            pre_copy(r, h).wait_send()
            fin_copy(r, h).wait_send()
    for i in range(hh + 2):
        x_copy(chip.at[0, 0], i).wait_send()
    for i in range(hh):
        y_copy(i).wait_send()


def fused(queries, keys, values, grad_out):
    tok, feat = queries.shape
    hh = feat // DH // 2
    factor = 1.0 / math.sqrt(DH * tok * lax.axis_size("ctx"))
    state = (DH, DH)
    sem = pltpu.SemaphoreType.DMA
    return pl.pallas_call(
        functools.partial(kernel, factor),
        out_shape=[jax.ShapeDtypeStruct((tok, feat), BF16)] * 4,
        in_specs=[pl.BlockSpec(memory_space=pltpu.HBM)] * 4,
        out_specs=[pl.BlockSpec(memory_space=pltpu.VMEM)] * 4,
        scratch_shapes=[
            pltpu.VMEM((4, 2, tok, feat // 2), BF16),
            pltpu.VMEM((2, 2, 2, hh, tok, DH), F32),
            pltpu.VMEM((2, hh) + state, F32),
            pltpu.VMEM((2, hh) + state, F32),
            pltpu.VMEM((2, hh) + state, F32),
            pltpu.VMEM((2, hh) + state, F32),
            pltpu.VMEM((hh + 2,) + state, F32),
            pltpu.VMEM((hh,) + state, F32),
            pltpu.VMEM((hh,) + state, F32),
            pltpu.VMEM((2, hh) + state, F32),
            pltpu.VMEM((2, hh) + state, F32),
            pltpu.VMEM((2, 2, hh) + state, BF16),
            sem((4, 2)),
            sem((2, hh)), sem((2, hh)),
            sem((hh + 2,)), sem((hh + 2,)),
            sem((hh,)), sem((hh,)),
            sem((2, hh)), sem((2, hh)),
        ],
        compiler_params=pltpu.CompilerParams(
            collective_id=0, has_side_effects=True, vmem_limit_bytes=52000 * 1024),
        name="lightning",
    )(queries, keys, values, grad_out)


def put_kernel(a, b, c, d, oa, ob, oc, od, sem):
    copies = []
    rows = a.shape[0] // PUT_PIECES
    for i, (src, dst) in enumerate(((a, oa), (b, ob), (c, oc), (d, od))):
        for j in range(PUT_PIECES):
            at = pl.ds(j * rows, rows)
            copies.append(pltpu.make_async_copy(src.at[at], dst.at[at], sem.at[i, j]))
    for copy in copies:
        copy.start()
    for copy in copies:
        copy.wait()


def put(arrays):
    return pl.pallas_call(
        put_kernel,
        out_shape=[jax.ShapeDtypeStruct(a.shape, a.dtype) for a in arrays],
        in_specs=[pl.BlockSpec(memory_space=pl.ANY)] * 4,
        out_specs=[pl.BlockSpec(memory_space=pl.ANY)] * 4,
        scratch_shapes=[pltpu.SemaphoreType.DMA((4, PUT_PIECES))],
        compiler_params=pltpu.CompilerParams(vmem_limit_bytes=1024 * 1024),
        name="put",
    )(*arrays)


def carried_in(value, axis, reverse):
    devices, index = (lax.axis_size(axis), lax.axis_index(axis))
    everything = lax.all_gather(value, axis)

    def hop(k, before):
        at = devices - 1 - k if reverse else k
        reached = at > index if reverse else at < index
        return jnp.where(reached, before + everything[at], before)

    return lax.fori_loop(0, devices, hop, jnp.zeros(value.shape, value.dtype))


def general(queries, keys, values, grad_out):
    tok_rows = queries.shape[0]
    feat_width = queries.shape[1]
    heads_here = feat_width // DH
    factor = 1.0 / math.sqrt(DH * tok_rows * lax.axis_size("ctx"))
    shape_three = (tok_rows, heads_here, DH)
    query_heads = queries.reshape(shape_three)
    key_heads = keys.reshape(shape_three)
    value_heads = values.reshape(shape_three)
    grad_heads = grad_out.reshape(shape_three)
    kv_local = jnp.einsum("shd,she->hde", key_heads, value_heads, preferred_element_type=F32)
    qg_local = jnp.einsum("shd,she->hde", query_heads, grad_heads, preferred_element_type=F32)
    kv_before = carried_in(kv_local, "ctx", False).astype(BF16)
    qg_after = carried_in(qg_local, "ctx", True).astype(BF16)
    row_ids = lax.broadcasted_iota(jnp.int32, (tok_rows, tok_rows), 0)
    col_ids = lax.broadcasted_iota(jnp.int32, (tok_rows, tok_rows), 1)
    causal = (col_ids <= row_ids)[None]
    raw_scores = jnp.einsum("shd,thd->hst", query_heads, key_heads, preferred_element_type=F32)
    scores = jnp.where(causal, raw_scores, 0.0).astype(BF16)
    attn = jnp.einsum("hst,thd->shd", scores, value_heads, preferred_element_type=F32)
    attn = attn + jnp.einsum("shd,hde->she", query_heads, kv_before, preferred_element_type=F32)
    raw_grad = jnp.einsum("she,the->hst", grad_heads, value_heads, preferred_element_type=F32)
    grad_scores = jnp.where(causal, raw_grad, 0.0).astype(BF16)
    grad_q = jnp.einsum("hst,thd->shd", grad_scores, key_heads, preferred_element_type=F32)
    grad_q = grad_q + jnp.einsum("she,hde->shd", grad_heads, kv_before, preferred_element_type=F32)
    grad_k = jnp.einsum("hst,shd->thd", grad_scores, query_heads, preferred_element_type=F32)
    grad_k = grad_k + jnp.einsum("she,hde->shd", value_heads, qg_after, preferred_element_type=F32)
    grad_v = jnp.einsum("hst,she->the", scores, grad_heads, preferred_element_type=F32)
    grad_v = grad_v + jnp.einsum("shd,hde->she", key_heads, qg_after, preferred_element_type=F32)

    def finish(array):
        return (array * factor).reshape(tok_rows, feat_width).astype(BF16)

    return (finish(attn), finish(grad_q), finish(grad_k), finish(grad_v))


def local(queries, keys, values, grad_out):
    if lax.axis_size("ctx") == 8 and queries.shape[1] == 8 * DH:
        return tuple(put(fused(queries, keys, values, grad_out)))
    return general(queries, keys, values, grad_out)


def solution(mesh):
    spec = P(("seq", "ctx"), "head")
    return jax.shard_map(local, mesh=mesh, in_specs=(spec,) * 4, out_specs=(spec,) * 4, check_vma=False)
```

profile of v0, /device:TPU:1, one launch (start us, length us, event | category | flops | bytes accessed | tf_op | source)
XLA Modules:
  0.0 19.9 jit_solution(3417042517202869231)
XLA Ops:
  0.6 17.5 %lightning.1 = (bf16[384,1024]{1,0:T(8,128)(2,1)S(1)}, bf16[384,1024]{1,0:T(8,128)(2,1)S(1)}, bf16[384,1024]{1,0:T(8,128)(2,1)S(1)}, bf16[384,1024]{1,0:T(8,128)(2,1)S(1)}) custom-call(bf16[384,1024]{1,0:T(8,128)(2,1)} %q_hbm.1, bf16[384,1024]{1,0:T(8,128)(2,1)} %k_hbm.1, bf16[384,1024]{1,0:T(8,128)(2,1)} %v_hbm.1, bf16[384,1024]{1,0:T(8,128)(2,1)} %g_hbm.1), custom_call_target="tpu_custom_call" | custom-call | tf_op jit(solution)/shard_map/lightning/pallas_call | solution.py:271
  18.1 1.8 %put.1 = (bf16[384,1024]{1,0:T(8,128)(2,1)}, bf16[384,1024]{1,0:T(8,128)(2,1)}, bf16[384,1024]{1,0:T(8,128)(2,1)}, bf16[384,1024]{1,0:T(8,128)(2,1)}) custom-call(bf16[384,1024]{1,0:T(8,128)(2,1)S(1)} %get-tuple-element.8.a, bf16[384,1024]{1,0:T(8,128)(2,1)S(1)} %get-tuple-element.9.b, bf16[384,1024]{1,0:T(8,128)(2,1)S(1)} %get-tuple-element.10.c, ...), custom_call_target="tpu_custom_call" | custom-call | tf_op jit(solution)/shard_map/put/pallas_call | solution.py:315
where the time goes:
time: 20.1 us; the launch traced here: 19.9 us
  Pallas kernels  19.2 us (96%)
  between operations  0.64 us (3%)
    pallas_call x1, Pallas kernels, fused(): pl.pallas_call(functools.partial(kernel, factor), out_shape=[jax.ShapeDty...  17.5 us
    pallas_call x1, Pallas kernels, put(): pl.pallas_call(put_kernel, out_shape=[jax.ShapeDtypeStruct(a.shape, a.dty...  1.76 us

commit v1 on v0

v1 whole, which is shorter than its diff:
```python
import functools
import math

import jax
import jax.numpy as jnp
from jax import lax
from jax.experimental import pallas as pl
from jax.experimental.pallas import tpu as pltpu
from jax.sharding import PartitionSpec as P

DH = 128
F32 = jnp.float32
BF16 = jnp.bfloat16
PUT_PIECES = 3


def dot_nn(a, b):
    return lax.dot_general(a, b, (((1,), (0,)), ((), ())), preferred_element_type=F32)


def dot_nt(a, b):
    return lax.dot_general(a, b, (((1,), (1,)), ((), ())), preferred_element_type=F32)


def dot_tn(a, b):
    return lax.dot_general(a, b, (((0,), (0,)), ((), ())), preferred_element_type=F32)


def kernel(factor, q_hbm, k_hbm, v_hbm, g_hbm, one_ref, two_ref,
           ops, acc, give, mine, pre, chip, xin, yin, xsum, fin, fin_in, states,
           in_sem, pre_s, pre_r, x_s, x_r, y_s, y_r, f_s, f_r):
    me = lax.axis_index("ctx")
    core = me % 2
    xb = (me // 2) % 2
    yb = me // 4
    end = xb == yb
    mid = xb != yb
    partner = me + 1 - 2 * core
    x_dev = me + 2 - 4 * xb
    y_dev = me + 4 - 8 * yb
    tok, feat = q_hbm.shape
    half = feat // 2
    hh = half // DH

    barrier = pltpu.get_barrier_semaphore()
    for dev in (partner, x_dev, y_dev):
        pl.semaphore_signal(barrier, inc=1, device_id={"ctx": dev}, device_id_type=pl.DeviceIdType.MESH)

    cols_of = (pl.multiple_of((1 - core) * half, half), pl.multiple_of(core * half, half))
    i_k, i_v, i_q, i_g = 2 * yb, 2 * yb + 1, 2 - 2 * yb, 3 - 2 * yb

    def fetch(op, slot, ref):
        return pltpu.make_async_copy(ref.at[:, pl.ds(cols_of[slot], half)], ops.at[op, slot], in_sem.at[op, slot])

    for role in (0, 1):
        @pl.when(yb == role)
        def _():
            refs = (k_hbm, v_hbm, q_hbm, g_hbm) if role == 0 else (q_hbm, g_hbm, k_hbm, v_hbm)
            for slot in (0, 1):
                for op in range(4):
                    fetch(op, slot, refs[op]).start()

    def remote(src, dst, ss, rs, dev):
        return pltpu.make_async_remote_copy(
            src_ref=src, dst_ref=dst, send_sem=ss, recv_sem=rs,
            device_id={"ctx": dev}, device_id_type=pl.DeviceIdType.MESH)

    def pre_copy(r, h):
        return remote(give.at[r, h], pre.at[r, h], pre_s.at[r, h], pre_r.at[r, h], partner)

    def x_copy(i, src=None):
        return remote(chip.at[0, 0] if src is None else src, xin.at[i], x_s.at[i], x_r.at[i], x_dev)

    def y_copy(i, src=None):
        return remote(chip.at[0, 0] if src is None else src, yin.at[i], y_s.at[i], y_r.at[i], y_dev)

    def fin_copy(r, h):
        return remote(fin.at[r, h], fin_in.at[r, h], f_s.at[r, h], f_r.at[r, h], partner)

    def wait_ops(r, slot):
        fetch(2 * r, slot, q_hbm).wait()
        fetch(2 * r + 1, slot, q_hbm).wait()

    def head(op, slot, h):
        return ops[op, slot, :, h * DH:(h + 1) * DH]

    def local_state(r, slot, h):
        return dot_tn(head(2 * r, slot, h), head(2 * r + 1, slot, h))

    def by_place(at_end, at_mid):
        pl.when(end)(at_end)
        pl.when(mid)(at_mid)

    order = (0, 2, 1, 3)
    via_y = {2: 4, 3: 5}
    via_x = {0: 4, 1: 5}

    for r in (0, 1):
        wait_ops(r, 0)
        for h in order:
            give[r, h] = local_state(r, 0, h)
        if r == 0:
            pl.semaphore_wait(barrier, 3)
        for h in order:
            pre_copy(r, h).start()
    for r in (0, 1):
        wait_ops(r, 1)
        for h in order:
            mine[r, h] = local_state(r, 1, h)

    def adds_pre(r):
        return (core + yb + r) % 2 == 1

    def finish_state(r, h, base):
        follows = adds_pre(r)
        zero = jnp.zeros((DH, DH), F32)
        own = jnp.where(follows, pre[r, h], zero)
        other = jnp.where(follows, zero, mine[r, h])
        if base is not None:
            own, other = own + base, other + base
        states[r, 1, h] = own.astype(BF16)
        fin[r, h] = other
        fin_copy(r, h).start()

    for h in order:
        pre_copy(0, h).wait_recv()
        chip[0, h] = mine[0, h] + pre[0, h]

        def send_end():
            x_copy(h, chip.at[0, h]).start()
            y_copy(h, chip.at[0, h]).start()

        def send_mid():
            if h in via_y:
                x_copy(via_y[h], chip.at[0, h]).start()
            y_copy(h, chip.at[0, h]).start()

        by_place(send_end, send_mid)
    for h in order:
        pre_copy(1, h).wait_recv()

    def early_end():
        for h in order:
            finish_state(0, h, None)

    def early_mid():
        for h in order:
            chip[1, h] = mine[1, h] + pre[1, h]

    by_place(early_end, early_mid)

    rows = lax.broadcasted_iota(jnp.int32, (tok, tok), 0)
    columns = lax.broadcasted_iota(jnp.int32, (tok, tok), 1)

    def intra(slot, *heads):
        for h in heads:
            q, k, v, g = head(i_q, slot, h), head(i_k, slot, h), head(i_v, slot, h), head(i_g, slot, h)
            causal = columns <= rows
            sc = jnp.where(causal, dot_nt(q, k), 0.0).astype(BF16)
            ds = jnp.where(causal, dot_nt(g, v), 0.0).astype(BF16)
            acc[0, 0, slot, h] = dot_nn(sc, v)
            acc[0, 1, slot, h] = dot_nn(ds, k)
            acc[1, 0, slot, h] = dot_tn(sc, g)
            acc[1, 1, slot, h] = dot_tn(ds, q)

    def apply(r, slot, *heads):
        kind = (yb + r) % 2
        for h in heads:
            state = states[r, slot, h]
            left, right = head(2 - 2 * r, slot, h), head(3 - 2 * r, slot, h)
            at = pl.ds(pl.multiple_of(cols_of[slot] + h * DH, DH), DH)
            one_ref[kind, :, at] = ((acc[kind, 0, slot, h] + dot_nn(left, state)) * factor).astype(BF16)
            two_ref[kind, :, at] = ((acc[kind, 1, slot, h] + dot_nt(right, state)) * factor).astype(BF16)

    def take_final(r, *heads):
        for h in heads:
            fin_copy(r, h).wait_recv()
            states[r, 0, h] = fin_in[r, h].astype(BF16)
        apply(r, 0, *heads)

    def far_sum(h):
        y_copy(h).wait_recv()
        xsum[h] = chip[1, h] + yin[h]
        x_copy(h, xsum.at[h]).start()

    def relay(hx, hy):
        y_copy(hx).wait_recv()
        x_copy(via_x[hx], yin.at[hx]).start()
        x_copy(via_y[hy]).wait_recv()
        y_copy(via_y[hy], xin.at[via_y[hy]]).start()

    def near_prefix(*heads):
        for h in heads:
            x_copy(h).wait_recv()
            finish_state(0, h, xin[h])

    def end_last(*heads):
        for h in heads:
            x_copy(h).wait_recv()
            if h in via_y:
                y_copy(h).wait_recv()
            finish_state(1, h, xin[h] + yin[h])

    def mid_last(*heads):
        for h in heads:
            if h in via_y:
                y_copy(via_y[h]).wait_recv()
                finish_state(1, h, yin[h] + yin[via_y[h]])
            else:
                x_copy(via_x[h]).wait_recv()
                finish_state(1, h, yin[h] + xin[via_x[h]])

    intra(0, 0, 1)
    intra(0, 2)
    pl.when(mid)(lambda: far_sum(0))
    intra(0, 3)
    intra(1, 0)
    by_place(lambda: relay(0, 2), lambda: far_sum(2))
    intra(1, 1)
    intra(1, 2)
    by_place(lambda: relay(1, 3), lambda: far_sum(1))
    intra(1, 3)
    pl.when(mid)(lambda: near_prefix(0, 2, 1))
    pl.when(mid)(lambda: far_sum(3))
    pl.when(mid)(lambda: near_prefix(3))
    apply(0, 1, 0, 2, 1, 3)
    pl.when(end)(lambda: end_last(0, 2))
    take_final(0, 0, 2, 1, 3)
    pl.when(mid)(lambda: mid_last(0, 2))
    apply(1, 1, 0, 2)
    take_final(1, 0, 2)
    by_place(lambda: end_last(1, 3), lambda: mid_last(1, 3))
    apply(1, 1, 1, 3)
    take_final(1, 1, 3)

    for r in (0, 1):
        for h in range(hh):
            pre_copy(r, h).wait_send()
            fin_copy(r, h).wait_send()
    for i in range(hh + 2):
        x_copy(i).wait_send()
    for i in range(hh):
        y_copy(i).wait_send()

    @pl.when(end)
    def _():
        for i in range(hh, hh + 2):
            y_copy(i).wait_send()


def fused(queries, keys, values, grad_out):
    tok, feat = queries.shape
    hh = feat // DH // 2
    factor = 1.0 / math.sqrt(DH * tok * lax.axis_size("ctx"))
    state = (DH, DH)
    sem = pltpu.SemaphoreType.DMA
    return pl.pallas_call(
        functools.partial(kernel, factor),
        out_shape=[pltpu.VMEM((2, tok, feat), BF16)] * 2,
        in_specs=[pl.BlockSpec(memory_space=pltpu.HBM)] * 4,
        out_specs=[pl.BlockSpec(memory_space=pltpu.VMEM)] * 2,
        scratch_shapes=[
            pltpu.VMEM((4, 2, tok, feat // 2), BF16),
            pltpu.VMEM((2, 2, 2, hh, tok, DH), F32),
            pltpu.VMEM((2, hh) + state, F32),
            pltpu.VMEM((2, hh) + state, F32),
            pltpu.VMEM((2, hh) + state, F32),
            pltpu.VMEM((2, hh) + state, F32),
            pltpu.VMEM((hh + 2,) + state, F32),
            pltpu.VMEM((hh + 2,) + state, F32),
            pltpu.VMEM((hh,) + state, F32),
            pltpu.VMEM((2, hh) + state, F32),
            pltpu.VMEM((2, hh) + state, F32),
            pltpu.VMEM((2, 2, hh) + state, BF16),
            sem((4, 2)),
            sem((2, hh)), sem((2, hh)),
            sem((hh + 2,)), sem((hh + 2,)),
            sem((hh + 2,)), sem((hh + 2,)),
            sem((2, hh)), sem((2, hh)),
        ],
        compiler_params=pltpu.CompilerParams(
            collective_id=0, has_side_effects=True, vmem_limit_bytes=52000 * 1024),
        name="lightning",
    )(queries, keys, values, grad_out)


def put_kernel(one, two, attn, gq, gv, gk, sem):
    copies = []
    rows = attn.shape[0] // PUT_PIECES
    for i, (src, dst) in enumerate(((one.at[0], attn), (two.at[0], gq), (one.at[1], gv), (two.at[1], gk))):
        for j in range(PUT_PIECES):
            at = pl.ds(j * rows, rows)
            copies.append(pltpu.make_async_copy(src.at[at], dst.at[at], sem.at[i, j]))
    for copy in copies:
        copy.start()
    for copy in copies:
        copy.wait()


def put(results):
    shape = jax.ShapeDtypeStruct(results[0].shape[1:], BF16)
    attn, gq, gv, gk = pl.pallas_call(
        put_kernel,
        out_shape=[shape] * 4,
        in_specs=[pl.BlockSpec(memory_space=pl.ANY)] * 2,
        out_specs=[pl.BlockSpec(memory_space=pl.ANY)] * 4,
        scratch_shapes=[pltpu.SemaphoreType.DMA((4, PUT_PIECES))],
        compiler_params=pltpu.CompilerParams(vmem_limit_bytes=1024 * 1024),
        name="put",
    )(*results)
    return attn, gq, gk, gv


def carried_in(value, axis, reverse):
    devices, index = (lax.axis_size(axis), lax.axis_index(axis))
    everything = lax.all_gather(value, axis)

    def hop(k, before):
        at = devices - 1 - k if reverse else k
        reached = at > index if reverse else at < index
        return jnp.where(reached, before + everything[at], before)

    return lax.fori_loop(0, devices, hop, jnp.zeros(value.shape, value.dtype))


def general(queries, keys, values, grad_out):
    tok_rows = queries.shape[0]
    feat_width = queries.shape[1]
    heads_here = feat_width // DH
    factor = 1.0 / math.sqrt(DH * tok_rows * lax.axis_size("ctx"))
    shape_three = (tok_rows, heads_here, DH)
    query_heads = queries.reshape(shape_three)
    key_heads = keys.reshape(shape_three)
    value_heads = values.reshape(shape_three)
    grad_heads = grad_out.reshape(shape_three)
    kv_local = jnp.einsum("shd,she->hde", key_heads, value_heads, preferred_element_type=F32)
    qg_local = jnp.einsum("shd,she->hde", query_heads, grad_heads, preferred_element_type=F32)
    kv_before = carried_in(kv_local, "ctx", False).astype(BF16)
    qg_after = carried_in(qg_local, "ctx", True).astype(BF16)
    row_ids = lax.broadcasted_iota(jnp.int32, (tok_rows, tok_rows), 0)
    col_ids = lax.broadcasted_iota(jnp.int32, (tok_rows, tok_rows), 1)
    causal = (col_ids <= row_ids)[None]
    raw_scores = jnp.einsum("shd,thd->hst", query_heads, key_heads, preferred_element_type=F32)
    scores = jnp.where(causal, raw_scores, 0.0).astype(BF16)
    attn = jnp.einsum("hst,thd->shd", scores, value_heads, preferred_element_type=F32)
    attn = attn + jnp.einsum("shd,hde->she", query_heads, kv_before, preferred_element_type=F32)
    raw_grad = jnp.einsum("she,the->hst", grad_heads, value_heads, preferred_element_type=F32)
    grad_scores = jnp.where(causal, raw_grad, 0.0).astype(BF16)
    grad_q = jnp.einsum("hst,thd->shd", grad_scores, key_heads, preferred_element_type=F32)
    grad_q = grad_q + jnp.einsum("she,hde->shd", grad_heads, kv_before, preferred_element_type=F32)
    grad_k = jnp.einsum("hst,shd->thd", grad_scores, query_heads, preferred_element_type=F32)
    grad_k = grad_k + jnp.einsum("she,hde->shd", value_heads, qg_after, preferred_element_type=F32)
    grad_v = jnp.einsum("hst,she->the", scores, grad_heads, preferred_element_type=F32)
    grad_v = grad_v + jnp.einsum("shd,hde->she", key_heads, qg_after, preferred_element_type=F32)

    def finish(array):
        return (array * factor).reshape(tok_rows, feat_width).astype(BF16)

    return (finish(attn), finish(grad_q), finish(grad_k), finish(grad_v))


def local(queries, keys, values, grad_out):
    if lax.axis_size("ctx") == 8 and queries.shape[1] == 8 * DH:
        return put(fused(queries, keys, values, grad_out))
    return general(queries, keys, values, grad_out)


def solution(mesh):
    spec = P(("seq", "ctx"), "head")
    return jax.shard_map(local, mesh=mesh, in_specs=(spec,) * 4, out_specs=(spec,) * 4, check_vma=False)
```

time: 20.1 us -> 20.6 us (1.025)
  Pallas kernels: 19.2 us -> 19.8 us
    pallas_call x2, Pallas kernels: 19.2 us -> 19.8 us  [the longest x1 18 us: fused(): pl.pallas_call(functools.partial(kernel, factor), out_shape=[pltpu.VMEM((...]
where the time goes in v1:
time: 20.6 us; the launch traced here: 20.4 us
  Pallas kernels  19.8 us (96%)
  between operations  0.64 us (3%)
    pallas_call x1, Pallas kernels, fused(): pl.pallas_call(functools.partial(kernel, factor), out_shape=[pltpu.VMEM((...  18 us
    pallas_call x1, Pallas kernels, put(): pl.pallas_call(put_kernel, out_shape=[shape] * 4, in_specs=[pl.BlockSpec(...  1.76 us

profile of v1, /device:TPU:1, one launch (start us, length us, event | category | flops | bytes accessed | tf_op | source)
XLA Modules:
  0.0 20.4 jit_solution(16498669050227266512)
XLA Ops:
  0.6 18.0 %lightning.1 = (bf16[2,384,1024]{2,1,0:T(8,128)(2,1)S(1)}, bf16[2,384,1024]{2,1,0:T(8,128)(2,1)S(1)}) custom-call(bf16[384,1024]{1,0:T(8,128)(2,1)} %q_hbm.1, bf16[384,1024]{1,0:T(8,128)(2,1)} %k_hbm.1, bf16[384,1024]{1,0:T(8,128)(2,1)} %v_hbm.1, bf16[384,1024]{1,0:T(8,128)(2,1)} %g_hbm.1), custom_call_target="tpu_custom_call" | custom-call | tf_op jit(solution)/shard_map/lightning/pallas_call | solution.py:257
  18.7 1.8 %put.1 = (bf16[384,1024]{1,0:T(8,128)(2,1)}, bf16[384,1024]{1,0:T(8,128)(2,1)}, bf16[384,1024]{1,0:T(8,128)(2,1)}, bf16[384,1024]{1,0:T(8,128)(2,1)}) custom-call(bf16[2,384,1024]{2,1,0:T(8,128)(2,1)S(1)} %get-tuple-element.10.one, bf16[2,384,1024]{2,1,0:T(8,128)(2,1)S(1)} %get-tuple-element.11.two), custom_call_target="tpu_custom_call" | custom-call | tf_op jit(solution)/shard_map/put/pallas_call | solution.py:302

commit v2 on v1

--- a/solution.py
+++ b/solution.py
@@ -27,7 +27,7 @@
 
 
 def kernel(factor, q_hbm, k_hbm, v_hbm, g_hbm, one_ref, two_ref,
-           ops, acc, give, mine, pre, chip, xin, yin, xsum, fin, fin_in, states,
+           ops, acc, give, mine, pre, chip, xin, yin, sums, fin, fin_in, states,
            in_sem, pre_s, pre_r, x_s, x_r, y_s, y_r, f_s, f_r):
     me = lax.axis_index("ctx")
     core = me % 2
@@ -92,8 +92,6 @@
         pl.when(mid)(at_mid)
 
     order = (0, 2, 1, 3)
-    via_y = {2: 4, 3: 5}
-    via_x = {0: 4, 1: 5}
 
     for r in (0, 1):
         wait_ops(r, 0)
@@ -127,27 +125,37 @@
         chip[0, h] = mine[0, h] + pre[0, h]
 
         def send_end():
+            (x_copy if h >= 2 else y_copy)(h, chip.at[0, h]).start()
+
+        def send_mid():
+            if h >= 2:
+                x_copy(h + 2, chip.at[0, h]).start()
+            else:
+                y_copy(h, chip.at[0, h]).start()
+
+        by_place(send_end, send_mid)
+
+    @pl.when(end)
+    def _():
+        for h in (0, 1):
             x_copy(h, chip.at[0, h]).start()
+        for h in (2, 3):
             y_copy(h, chip.at[0, h]).start()
 
-        def send_mid():
-            if h in via_y:
-                x_copy(via_y[h], chip.at[0, h]).start()
-            y_copy(h, chip.at[0, h]).start()
-
-        by_place(send_end, send_mid)
-    for h in order:
+    for h in (2, 3, 0, 1):
         pre_copy(1, h).wait_recv()
 
-    def early_end():
-        for h in order:
+        def far_mid():
+            chip[1, h] = mine[1, h] + pre[1, h]
+            if h >= 2:
+                x_copy(h, chip.at[1, h]).start()
+
+        pl.when(mid)(far_mid)
+
+    @pl.when(end)
+    def _():
+        for h in range(hh):
             finish_state(0, h, None)
-
-    def early_mid():
-        for h in order:
-            chip[1, h] = mine[1, h] + pre[1, h]
-
-    by_place(early_end, early_mid)
 
     rows = lax.broadcasted_iota(jnp.int32, (tok, tok), 0)
     columns = lax.broadcasted_iota(jnp.int32, (tok, tok), 1)
@@ -178,60 +186,77 @@
             states[r, 0, h] = fin_in[r, h].astype(BF16)
         apply(r, 0, *heads)
 
-    def far_sum(h):
-        y_copy(h).wait_recv()
-        xsum[h] = chip[1, h] + yin[h]
-        x_copy(h, xsum.at[h]).start()
-
-    def relay(hx, hy):
-        y_copy(hx).wait_recv()
-        x_copy(via_x[hx], yin.at[hx]).start()
-        x_copy(via_y[hy]).wait_recv()
-        y_copy(via_y[hy], xin.at[via_y[hy]]).start()
+    def mid_sums(hx, hy):
+        x_copy(hx).wait_recv()
+        sums[hx] = chip[0, hx] + xin[hx]
+        y_copy(hx, sums.at[hx]).start()
+        y_copy(hy).wait_recv()
+        sums[hy] = chip[1, hy] + yin[hy]
+        x_copy(hy, sums.at[hy]).start()
+
+    def relay(hy, hx):
+        y_copy(hy).wait_recv()
+        x_copy(4 + hy, yin.at[hy]).start()
+        x_copy(2 + hx).wait_recv()
+        y_copy(2 + hx, xin.at[2 + hx]).start()
 
     def near_prefix(*heads):
         for h in heads:
+            if h < 2:
+                x_copy(h).wait_recv()
+            finish_state(0, h, xin[h])
+
+    def end_last(*heads):
+        for h in heads:
             x_copy(h).wait_recv()
-            finish_state(0, h, xin[h])
-
-    def end_last(*heads):
-        for h in heads:
-            x_copy(h).wait_recv()
-            if h in via_y:
+            if h >= 2:
                 y_copy(h).wait_recv()
             finish_state(1, h, xin[h] + yin[h])
 
     def mid_last(*heads):
         for h in heads:
-            if h in via_y:
-                y_copy(via_y[h]).wait_recv()
-                finish_state(1, h, yin[h] + yin[via_y[h]])
+            if h < 2:
+                x_copy(4 + h).wait_recv()
+                finish_state(1, h, yin[h] + xin[4 + h])
             else:
-                x_copy(via_x[h]).wait_recv()
-                finish_state(1, h, yin[h] + xin[via_x[h]])
+                y_copy(h).wait_recv()
+                y_copy(2 + h).wait_recv()
+                finish_state(1, h, yin[h] + yin[2 + h])
+
+    def end_tail():
+        apply(0, 1, *order)
+        take_final(0, *order)
+        end_last(2, 3)
+        apply(1, 1, 2, 3)
+        end_last(0)
+        take_final(1, 2, 3)
+        apply(1, 1, 0)
+        end_last(1)
+        apply(1, 1, 1)
+        take_final(1, 0, 1)
+
+    def mid_tail():
+        near_prefix(1)
+        apply(0, 1, *order)
+        take_final(0, *order)
+        mid_last(0, 2)
+        apply(1, 1, 0, 2)
+        take_final(1, 0, 2)
+        mid_last(1, 3)
+        apply(1, 1, 1, 3)
+        take_final(1, 1, 3)
 
     intra(0, 0, 1)
     intra(0, 2)
-    pl.when(mid)(lambda: far_sum(0))
+    by_place(lambda: relay(0, 2), lambda: mid_sums(2, 0))
     intra(0, 3)
+    pl.when(mid)(lambda: mid_sums(3, 1))
     intra(1, 0)
-    by_place(lambda: relay(0, 2), lambda: far_sum(2))
+    by_place(lambda: relay(1, 3), lambda: near_prefix(2, 3))
     intra(1, 1)
-    intra(1, 2)
-    by_place(lambda: relay(1, 3), lambda: far_sum(1))
-    intra(1, 3)
-    pl.when(mid)(lambda: near_prefix(0, 2, 1))
-    pl.when(mid)(lambda: far_sum(3))
-    pl.when(mid)(lambda: near_prefix(3))
-    apply(0, 1, 0, 2, 1, 3)
-    pl.when(end)(lambda: end_last(0, 2))
-    take_final(0, 0, 2, 1, 3)
-    pl.when(mid)(lambda: mid_last(0, 2))
-    apply(1, 1, 0, 2)
-    take_final(1, 0, 2)
-    by_place(lambda: end_last(1, 3), lambda: mid_last(1, 3))
-    apply(1, 1, 1, 3)
-    take_final(1, 1, 3)
+    pl.when(mid)(lambda: near_prefix(0))
+    intra(1, 2, 3)
+    by_place(end_tail, mid_tail)
 
     for r in (0, 1):
         for h in range(hh):

time: 20.6 us -> 19.4 us (0.942)
  Pallas kernels: 19.8 us -> 18.6 us
    pallas_call x1, Pallas kernels: 18 us -> 16.8 us  [fused(): pl.pallas_call(functools.partial(kernel, factor), out_shape=[pltpu.VMEM((...]
where the time goes in v2:
time: 19.4 us; the launch traced here: 19.2 us
  Pallas kernels  18.6 us (96%)
  between operations  0.64 us (3%)
    pallas_call x1, Pallas kernels, fused(): pl.pallas_call(functools.partial(kernel, factor), out_shape=[pltpu.VMEM((...  16.8 us
    pallas_call x1, Pallas kernels, put(): pl.pallas_call(put_kernel, out_shape=[shape] * 4, in_specs=[pl.BlockSpec(...  1.76 us

profile of v2, /device:TPU:1, one launch (start us, length us, event | category | flops | bytes accessed | tf_op | source)
XLA Modules:
  0.0 19.2 jit_solution(15618589898318994145)
XLA Ops:
  0.6 16.8 %lightning.1 = (bf16[2,384,1024]{2,1,0:T(8,128)(2,1)S(1)}, bf16[2,384,1024]{2,1,0:T(8,128)(2,1)S(1)}) custom-call(bf16[384,1024]{1,0:T(8,128)(2,1)} %q_hbm.1, bf16[384,1024]{1,0:T(8,128)(2,1)} %k_hbm.1, bf16[384,1024]{1,0:T(8,128)(2,1)} %v_hbm.1, bf16[384,1024]{1,0:T(8,128)(2,1)} %g_hbm.1), custom_call_target="tpu_custom_call" | custom-call | tf_op jit(solution)/shard_map/lightning/pallas_call | solution.py:282
  17.5 1.8 %put.1 = (bf16[384,1024]{1,0:T(8,128)(2,1)}, bf16[384,1024]{1,0:T(8,128)(2,1)}, bf16[384,1024]{1,0:T(8,128)(2,1)}, bf16[384,1024]{1,0:T(8,128)(2,1)}) custom-call(bf16[2,384,1024]{2,1,0:T(8,128)(2,1)S(1)} %get-tuple-element.10.one, bf16[2,384,1024]{2,1,0:T(8,128)(2,1)S(1)} %get-tuple-element.11.two), custom_call_target="tpu_custom_call" | custom-call | tf_op jit(solution)/shard_map/put/pallas_call | solution.py:327

commit v3 on v2

--- a/solution.py
+++ b/solution.py
@@ -11,7 +11,6 @@
 DH = 128
 F32 = jnp.float32
 BF16 = jnp.bfloat16
-PUT_PIECES = 3
 
 
 def dot_nn(a, b):
@@ -50,7 +49,7 @@
     i_k, i_v, i_q, i_g = 2 * yb, 2 * yb + 1, 2 - 2 * yb, 3 - 2 * yb
 
     def fetch(op, slot, ref):
-        return pltpu.make_async_copy(ref.at[:, pl.ds(cols_of[slot], half)], ops.at[op, slot], in_sem.at[op, slot])
+        return pltpu.make_async_copy(ref.at[:, pl.ds(cols_of[slot], half)], ops.at[op, slot], in_sem.at[op // 2, slot])
 
     for role in (0, 1):
         @pl.when(yb == role)
@@ -66,20 +65,20 @@
             device_id={"ctx": dev}, device_id_type=pl.DeviceIdType.MESH)
 
     def pre_copy(r, h):
-        return remote(give.at[r, h], pre.at[r, h], pre_s.at[r, h], pre_r.at[r, h], partner)
+        return remote(give.at[r, h], pre.at[r, h], pre_s, pre_r.at[r, h], partner)
 
     def x_copy(i, src=None):
-        return remote(chip.at[0, 0] if src is None else src, xin.at[i], x_s.at[i], x_r.at[i], x_dev)
+        return remote(chip.at[0, 0] if src is None else src, xin.at[i], x_s, x_r.at[i], x_dev)
 
     def y_copy(i, src=None):
-        return remote(chip.at[0, 0] if src is None else src, yin.at[i], y_s.at[i], y_r.at[i], y_dev)
+        return remote(chip.at[0, 0] if src is None else src, yin.at[i], y_s, y_r.at[i], y_dev)
 
     def fin_copy(r, h):
-        return remote(fin.at[r, h], fin_in.at[r, h], f_s.at[r, h], f_r.at[r, h], partner)
+        return remote(fin.at[r, h], fin_in.at[r, h], f_s, f_r.at[r, h], partner)
 
     def wait_ops(r, slot):
-        fetch(2 * r, slot, q_hbm).wait()
-        fetch(2 * r + 1, slot, q_hbm).wait()
+        both = ops.at[2 * r:2 * r + 2, slot]
+        pltpu.make_async_copy(both, both, in_sem.at[r, slot]).wait()
 
     def head(op, slot, h):
         return ops[op, slot, :, h * DH:(h + 1) * DH]
@@ -238,12 +237,12 @@
     def mid_tail():
         near_prefix(1)
         apply(0, 1, *order)
-        take_final(0, *order)
         mid_last(0, 2)
         apply(1, 1, 0, 2)
-        take_final(1, 0, 2)
+        take_final(0, *order)
         mid_last(1, 3)
         apply(1, 1, 1, 3)
+        take_final(1, 0, 2)
         take_final(1, 1, 3)
 
     intra(0, 0, 1)
@@ -258,19 +257,15 @@
     intra(1, 2, 3)
     by_place(end_tail, mid_tail)
 
-    for r in (0, 1):
-        for h in range(hh):
-            pre_copy(r, h).wait_send()
-            fin_copy(r, h).wait_send()
-    for i in range(hh + 2):
-        x_copy(i).wait_send()
-    for i in range(hh):
-        y_copy(i).wait_send()
-
-    @pl.when(end)
-    def _():
-        for i in range(hh, hh + 2):
-            y_copy(i).wait_send()
+    remote(give, pre, pre_s, pre_r.at[0, 0], partner).wait_send()
+    remote(fin, fin_in, f_s, f_r.at[0, 0], partner).wait_send()
+    remote(xin, xin, x_s, x_r.at[0], x_dev).wait_send()
+
+    def sent_y(count):
+        part = yin.at[0:count]
+        remote(part, part, y_s, y_r.at[0], y_dev).wait_send()
+
+    by_place(lambda: sent_y(hh + 2), lambda: sent_y(hh))
 
 
 def fused(queries, keys, values, grad_out):
@@ -297,11 +292,11 @@
             pltpu.VMEM((2, hh) + state, F32),
             pltpu.VMEM((2, hh) + state, F32),
             pltpu.VMEM((2, 2, hh) + state, BF16),
-            sem((4, 2)),
-            sem((2, hh)), sem((2, hh)),
-            sem((hh + 2,)), sem((hh + 2,)),
-            sem((hh + 2,)), sem((hh + 2,)),
-            sem((2, hh)), sem((2, hh)),
+            sem((2, 2)),
+            sem, sem((2, hh)),
+            sem, sem((hh + 2,)),
+            sem, sem((hh + 2,)),
+            sem, sem((2, hh)),
         ],
         compiler_params=pltpu.CompilerParams(
             collective_id=0, has_side_effects=True, vmem_limit_bytes=52000 * 1024),
@@ -310,12 +305,9 @@
 
 
 def put_kernel(one, two, attn, gq, gv, gk, sem):
-    copies = []
-    rows = attn.shape[0] // PUT_PIECES
-    for i, (src, dst) in enumerate(((one.at[0], attn), (two.at[0], gq), (one.at[1], gv), (two.at[1], gk))):
-        for j in range(PUT_PIECES):
-            at = pl.ds(j * rows, rows)
-            copies.append(pltpu.make_async_copy(src.at[at], dst.at[at], sem.at[i, j]))
+    copies = [
+        pltpu.make_async_copy(src, dst, sem.at[i])
+        for i, (src, dst) in enumerate(((one.at[0], attn), (two.at[0], gq), (one.at[1], gv), (two.at[1], gk)))]
     for copy in copies:
         copy.start()
     for copy in copies:
@@ -329,7 +321,7 @@
         out_shape=[shape] * 4,
         in_specs=[pl.BlockSpec(memory_space=pl.ANY)] * 2,
         out_specs=[pl.BlockSpec(memory_space=pl.ANY)] * 4,
-        scratch_shapes=[pltpu.SemaphoreType.DMA((4, PUT_PIECES))],
+        scratch_shapes=[pltpu.SemaphoreType.DMA((4,))],
         compiler_params=pltpu.CompilerParams(vmem_limit_bytes=1024 * 1024),
         name="put",
     )(*results)

time: 19.4 us -> 19 us (0.979)
  Pallas kernels: 18.6 us -> 18.2 us
    pallas_call x1, Pallas kernels: 16.8 us -> 16.5 us  [fused(): pl.pallas_call(functools.partial(kernel, factor), out_shape=[pltpu.VMEM((...]
where the time goes in v3:
time: 19 us; the launch traced here: 18.9 us
  Pallas kernels  18.2 us (96%)
  between operations  0.64 us (3%)
    pallas_call x1, Pallas kernels, fused(): pl.pallas_call(functools.partial(kernel, factor), out_shape=[pltpu.VMEM((...  16.5 us
    pallas_call x1, Pallas kernels, put(): pl.pallas_call(put_kernel, out_shape=[shape] * 4, in_specs=[pl.BlockSpec(...  1.69 us

profile of v3, /device:TPU:1, one launch (start us, length us, event | category | flops | bytes accessed | tf_op | source)
XLA Modules:
  0.0 18.9 jit_solution(16136534803280251674)
XLA Ops:
  0.6 16.5 %lightning.1 = (bf16[2,384,1024]{2,1,0:T(8,128)(2,1)S(1)}, bf16[2,384,1024]{2,1,0:T(8,128)(2,1)S(1)}) custom-call(bf16[384,1024]{1,0:T(8,128)(2,1)} %q_hbm.1, bf16[384,1024]{1,0:T(8,128)(2,1)} %k_hbm.1, bf16[384,1024]{1,0:T(8,128)(2,1)} %v_hbm.1, bf16[384,1024]{1,0:T(8,128)(2,1)} %g_hbm.1), custom_call_target="tpu_custom_call" | custom-call | tf_op jit(solution)/shard_map/lightning/pallas_call | solution.py:277
  17.2 1.7 %put.1 = (bf16[384,1024]{1,0:T(8,128)(2,1)}, bf16[384,1024]{1,0:T(8,128)(2,1)}, bf16[384,1024]{1,0:T(8,128)(2,1)}, bf16[384,1024]{1,0:T(8,128)(2,1)}) custom-call(bf16[2,384,1024]{2,1,0:T(8,128)(2,1)S(1)} %get-tuple-element.10.one, bf16[2,384,1024]{2,1,0:T(8,128)(2,1)S(1)} %get-tuple-element.11.two), custom_call_target="tpu_custom_call" | custom-call | tf_op jit(solution)/shard_map/put/pallas_call | solution.py:319
